TPU v7x, 512 devices: a whole 4x4x16 slice. The times are simulated.
512 devices in a mesh: img: 32 (over z, y_hi), comp: 2 (over y_lo), ref: 8 (over x, core).
Axes of the slice: x: 4, y: 4 (y_hi: 2, y_lo: 2; y = y_hi * 2 + y_lo), z: 16, core: 2. Of those that a mesh axis runs over, the one named last changes fastest.
Arguments:
- images: float32 [3072, 16384], P('img', 'comp'), may hold values from -24 to 24
- references: float32 [2048, 16384], P(('img', 'ref'), 'comp'), may hold values from -0.140625 to 0.140625
Outputs:
- weighted_sums: float32 [2048, 16384], P(('img', 'ref'), 'comp')
All inputs are finite; a program needn't handle non-finite values.
Results may differ from a plain program's by a relative error of at most 0.0003.
Values sent between devices are 32-bit elements; how exact they have to be, the bound alone decides.
No kernel may reach another device: no remote copies, remote signals or barrier semaphores. Data moves between devices by JAX's collectives and lax.ppermute only.
A program may use at most 64 MiB of HBM per device.

v0:
```python
import jax
import jax.numpy as jnp
from jax import lax
from jax.sharding import PartitionSpec as P


def joined(x, axis, combine):
    everything = jax.tree.map(lambda part: lax.all_gather(part, axis), x)
    leading = jax.tree.map(lambda part: part[0], everything)

    def lap(k, so_far):
        return combine(so_far, jax.tree.map(lambda part: part[k], everything))

    return lax.fori_loop(1, lax.axis_size(axis), lap, leading)


def passed_along(value, axis, steps):
    count = lax.axis_size(axis)
    pairs = [(source, (source + steps) % count) for source in range(count)]
    return lax.ppermute(value, axis, pairs)


def combine(earlier, later):
    largest = jnp.maximum(earlier[0], later[0])
    totals = earlier[1] * jnp.exp(earlier[0] - largest) + later[1] * jnp.exp(later[0] - largest)
    return (largest, totals)


def softmax_parts(scores):
    largest = jnp.max(scores, axis=1)
    totals = jnp.sum(jnp.exp(scores - largest[:, None]), axis=1)
    return (largest, totals)


def shards(images, references):
    highest = lax.Precision.HIGHEST
    ref_rows = references.shape[0]
    count_img = lax.axis_size("img")
    piece = lax.all_gather(references, "img", axis=0, tiled=True)
    piece_scores = jnp.dot(images, piece.T, precision=highest, preferred_element_type=jnp.float32)
    piece_scores = piece_scores - 0.5 * jnp.sum(piece * piece, axis=1)[None, :]
    scores = lax.psum(piece_scores, "comp")
    largest, totals = softmax_parts(scores)
    largest, totals = joined((largest, totals), "ref", combine)
    posterior = jnp.exp(scores - largest[:, None]) / totals[:, None]
    weighted = jnp.dot(posterior.T, images, precision=highest, preferred_element_type=jnp.float32)
    position = lax.axis_index("img")

    def slice_for(offset):
        block = (position + offset) % count_img * ref_rows
        return lax.dynamic_slice_in_dim(weighted, block, ref_rows, 0)

    def forward_turn(turn_index, carried):
        moved = passed_along(carried, "img", 1)
        return moved + slice_for(-1 - turn_index)

    result = lax.fori_loop(1, count_img, forward_turn, slice_for(-1))
    return result


def solution(mesh):
    return jax.shard_map(
        shards,
        mesh=mesh,
        in_specs=(P("img", "comp"), P(("img", "ref"), "comp")),
        out_specs=P(("img", "ref"), "comp"),
        check_vma=False,
    )
```

profile of v0, /device:TPU:6, one launch (start us, length us, event | category | flops | bytes accessed | tf_op | source)
XLA Modules:
  0.0 739.4 jit_solution(3567135965348315679)
XLA Ops:
  7.3 199.0 %all-gather.4.cloned.1.call-done = f32[256,8192]{1,0:T(8,128)} async-done(((f32[8,8192]{1,0:T(8,128)}), f32[256,8192]{1,0:T(8,128)}) %all-gather.4.cloned.1.call-update) | async-done | bytes 8388624 | tf_op jit(solution)/shard_map/all_gather | solution.py:39
  222.6 36.0 %all-reduce.5.cloned.1.call-done = f32[96,256]{1,0:T(8,128)} async-done(((f32[96,256]{1,0:T(8,128)}), f32[96,256]{1,0:T(8,128)}) %all-reduce.5.cloned.1.call-update) | async-done | bytes 98320 | tf_op jit(solution)/shard_map/psum | solution.py:42
  261.2 10.4 %all-reduce.2 = (f32[768]{0:T(1024)S(1)}, f32[768]{0:T(1024)S(1)}) all-reduce(f32[768]{0:T(1024)S(1)} %dynamic-update-slice, f32[768]{0:T(1024)S(1)} %dynamic-update-slice.1), channel_id=2, replica_groups=mesh['img'=32,'comp'=2,'ref'=8] {'ref'}, use_global_device_ids=true, to_apply=%add | all-reduce | flops 1536 | bytes 12288
  283.4 449.2 %while.33 = (s32[]{:T(128)}, f32[8,8192]{1,0:T(8,128)}, s32[]{:T(128)}, f32[256,8192]{1,0:T(8,128)}, s32[]{:T(128)}, /*index=5*/s32[]{:T(128)}, s32[]{:T(128)}, ...) while((s32[]{:T(128)}, f32[8,8192]{1,0:T(8,128)}, s32[]{:T(128)}, f32[256,8192]{1,0:T(8,128)}, s32[]{:T(128)}, ...), condition=%wide.region_7.8_spmd, body=%wide.region_6.7_spmd.sunk | while | flops 65555 | bytes 1835340 | solution.py:57
  288.0 10.3 %collective-permute-done = f32[8,8192]{1,0:T(8,128)S(1)} collective-permute-done((f32[8,8192]{1,0:T(8,128)}, f32[8,8192]{1,0:T(8,128)S(1)}, u32[]{:S(2)}, u32[]{:S(2)}) %collective-permute-start) | collective-permute-done | bytes 262176 | tf_op jit(solution)/shard_map/while/body/eval_jaxpr/ppermute | solution.py:20
  302.2 12.0 %collective-permute-done = f32[8,8192]{1,0:T(8,128)S(1)} collective-permute-done((f32[8,8192]{1,0:T(8,128)}, f32[8,8192]{1,0:T(8,128)S(1)}, u32[]{:S(2)}, u32[]{:S(2)}) %collective-permute-start) | collective-permute-done | bytes 262176 | tf_op jit(solution)/shard_map/while/body/eval_jaxpr/ppermute | solution.py:20
  317.9 11.5 %collective-permute-done = f32[8,8192]{1,0:T(8,128)S(1)} collective-permute-done((f32[8,8192]{1,0:T(8,128)}, f32[8,8192]{1,0:T(8,128)S(1)}, u32[]{:S(2)}, u32[]{:S(2)}) %collective-permute-start) | collective-permute-done | bytes 262176 | tf_op jit(solution)/shard_map/while/body/eval_jaxpr/ppermute | solution.py:20
  333.0 10.6 %collective-permute-done = f32[8,8192]{1,0:T(8,128)S(1)} collective-permute-done((f32[8,8192]{1,0:T(8,128)}, f32[8,8192]{1,0:T(8,128)S(1)}, u32[]{:S(2)}, u32[]{:S(2)}) %collective-permute-start) | collective-permute-done | bytes 262176 | tf_op jit(solution)/shard_map/while/body/eval_jaxpr/ppermute | solution.py:20
  347.2 10.1 %collective-permute-done = f32[8,8192]{1,0:T(8,128)S(1)} collective-permute-done((f32[8,8192]{1,0:T(8,128)}, f32[8,8192]{1,0:T(8,128)S(1)}, u32[]{:S(2)}, u32[]{:S(2)}) %collective-permute-start) | collective-permute-done | bytes 262176 | tf_op jit(solution)/shard_map/while/body/eval_jaxpr/ppermute | solution.py:20
  416.0 10.1 %collective-permute-done = f32[8,8192]{1,0:T(8,128)S(1)} collective-permute-done((f32[8,8192]{1,0:T(8,128)}, f32[8,8192]{1,0:T(8,128)S(1)}, u32[]{:S(2)}, u32[]{:S(2)}) %collective-permute-start) | collective-permute-done | bytes 262176 | tf_op jit(solution)/shard_map/while/body/eval_jaxpr/ppermute | solution.py:20
  429.8 10.4 %collective-permute-done = f32[8,8192]{1,0:T(8,128)S(1)} collective-permute-done((f32[8,8192]{1,0:T(8,128)}, f32[8,8192]{1,0:T(8,128)S(1)}, u32[]{:S(2)}, u32[]{:S(2)}) %collective-permute-start) | collective-permute-done | bytes 262176 | tf_op jit(solution)/shard_map/while/body/eval_jaxpr/ppermute | solution.py:20
  443.8 11.6 %collective-permute-done = f32[8,8192]{1,0:T(8,128)S(1)} collective-permute-done((f32[8,8192]{1,0:T(8,128)}, f32[8,8192]{1,0:T(8,128)S(1)}, u32[]{:S(2)}, u32[]{:S(2)}) %collective-permute-start) | collective-permute-done | bytes 262176 | tf_op jit(solution)/shard_map/while/body/eval_jaxpr/ppermute | solution.py:20
  459.0 12.7 %collective-permute-done = f32[8,8192]{1,0:T(8,128)S(1)} collective-permute-done((f32[8,8192]{1,0:T(8,128)}, f32[8,8192]{1,0:T(8,128)S(1)}, u32[]{:S(2)}, u32[]{:S(2)}) %collective-permute-start) | collective-permute-done | bytes 262176 | tf_op jit(solution)/shard_map/while/body/eval_jaxpr/ppermute | solution.py:20
  475.3 12.1 %collective-permute-done = f32[8,8192]{1,0:T(8,128)S(1)} collective-permute-done((f32[8,8192]{1,0:T(8,128)}, f32[8,8192]{1,0:T(8,128)S(1)}, u32[]{:S(2)}, u32[]{:S(2)}) %collective-permute-start) | collective-permute-done | bytes 262176 | tf_op jit(solution)/shard_map/while/body/eval_jaxpr/ppermute | solution.py:20
  491.0 11.2 %collective-permute-done = f32[8,8192]{1,0:T(8,128)S(1)} collective-permute-done((f32[8,8192]{1,0:T(8,128)}, f32[8,8192]{1,0:T(8,128)S(1)}, u32[]{:S(2)}, u32[]{:S(2)}) %collective-permute-start) | collective-permute-done | bytes 262176 | tf_op jit(solution)/shard_map/while/body/eval_jaxpr/ppermute | solution.py:20
  505.9 10.4 %collective-permute-done = f32[8,8192]{1,0:T(8,128)S(1)} collective-permute-done((f32[8,8192]{1,0:T(8,128)}, f32[8,8192]{1,0:T(8,128)S(1)}, u32[]{:S(2)}, u32[]{:S(2)}) %collective-permute-start) | collective-permute-done | bytes 262176 | tf_op jit(solution)/shard_map/while/body/eval_jaxpr/ppermute | solution.py:20
  519.9 10.1 %collective-permute-done = f32[8,8192]{1,0:T(8,128)S(1)} collective-permute-done((f32[8,8192]{1,0:T(8,128)}, f32[8,8192]{1,0:T(8,128)S(1)}, u32[]{:S(2)}, u32[]{:S(2)}) %collective-permute-start) | collective-permute-done | bytes 262176 | tf_op jit(solution)/shard_map/while/body/eval_jaxpr/ppermute | solution.py:20
  533.7 10.1 %collective-permute-done = f32[8,8192]{1,0:T(8,128)S(1)} collective-permute-done((f32[8,8192]{1,0:T(8,128)}, f32[8,8192]{1,0:T(8,128)S(1)}, u32[]{:S(2)}, u32[]{:S(2)}) %collective-permute-start) | collective-permute-done | bytes 262176 | tf_op jit(solution)/shard_map/while/body/eval_jaxpr/ppermute | solution.py:20
  602.4 10.7 %collective-permute-done = f32[8,8192]{1,0:T(8,128)S(1)} collective-permute-done((f32[8,8192]{1,0:T(8,128)}, f32[8,8192]{1,0:T(8,128)S(1)}, u32[]{:S(2)}, u32[]{:S(2)}) %collective-permute-start) | collective-permute-done | bytes 262176 | tf_op jit(solution)/shard_map/while/body/eval_jaxpr/ppermute | solution.py:20
  616.7 11.8 %collective-permute-done = f32[8,8192]{1,0:T(8,128)S(1)} collective-permute-done((f32[8,8192]{1,0:T(8,128)}, f32[8,8192]{1,0:T(8,128)S(1)}, u32[]{:S(2)}, u32[]{:S(2)}) %collective-permute-start) | collective-permute-done | bytes 262176 | tf_op jit(solution)/shard_map/while/body/eval_jaxpr/ppermute | solution.py:20
  632.1 12.9 %collective-permute-done = f32[8,8192]{1,0:T(8,128)S(1)} collective-permute-done((f32[8,8192]{1,0:T(8,128)}, f32[8,8192]{1,0:T(8,128)S(1)}, u32[]{:S(2)}, u32[]{:S(2)}) %collective-permute-start) | collective-permute-done | bytes 262176 | tf_op jit(solution)/shard_map/while/body/eval_jaxpr/ppermute | solution.py:20
  648.7 12.1 %collective-permute-done = f32[8,8192]{1,0:T(8,128)S(1)} collective-permute-done((f32[8,8192]{1,0:T(8,128)}, f32[8,8192]{1,0:T(8,128)S(1)}, u32[]{:S(2)}, u32[]{:S(2)}) %collective-permute-start) | collective-permute-done | bytes 262176 | tf_op jit(solution)/shard_map/while/body/eval_jaxpr/ppermute | solution.py:20
  664.4 11.2 %collective-permute-done = f32[8,8192]{1,0:T(8,128)S(1)} collective-permute-done((f32[8,8192]{1,0:T(8,128)}, f32[8,8192]{1,0:T(8,128)S(1)}, u32[]{:S(2)}, u32[]{:S(2)}) %collective-permute-start) | collective-permute-done | bytes 262176 | tf_op jit(solution)/shard_map/while/body/eval_jaxpr/ppermute | solution.py:20
  679.3 10.4 %collective-permute-done = f32[8,8192]{1,0:T(8,128)S(1)} collective-permute-done((f32[8,8192]{1,0:T(8,128)}, f32[8,8192]{1,0:T(8,128)S(1)}, u32[]{:S(2)}, u32[]{:S(2)}) %collective-permute-start) | collective-permute-done | bytes 262176 | tf_op jit(solution)/shard_map/while/body/eval_jaxpr/ppermute | solution.py:20
  (107 shorter events, 256.6 us)
Async XLA Ops:
  6.5 199.7 %all-gather.4.cloned.1.call-start = ((), (), s32[]{:S(2)}) async-start(), calls=%async_computation | async-start | bytes 8650752 | tf_op jit(solution)/shard_map/all_gather | solution.py:39
  7.3 251.4 %all-reduce.5.cloned.1.call-start = ((), (), s32[]{:S(2)}) async-start(), calls=%async_computation.1 | async-start | bytes 196608 | tf_op jit(solution)/shard_map/psum | solution.py:42
  283.4 14.9 %collective-permute-start = (f32[8,8192]{1,0:T(8,128)}, f32[8,8192]{1,0:T(8,128)S(1)}, u32[]{:S(2)}, u32[]{:S(2)}) collective-permute-start(f32[8,8192]{1,0:T(8,128)} %get-tuple-element.370), channel_id=1, source_target_pairs={{0,16},{16,32},{32,48},{48,64},{64,80},{80,96},{96,112},{112,128},... | collective-permute-start | bytes 786440 | tf_op jit(solution)/shard_map/while/body/eval_jaxpr/ppermute | solution.py:20
  300.0 14.3 %collective-permute-start = (f32[8,8192]{1,0:T(8,128)}, f32[8,8192]{1,0:T(8,128)S(1)}, u32[]{:S(2)}, u32[]{:S(2)}) collective-permute-start(f32[8,8192]{1,0:T(8,128)} %get-tuple-element.370), channel_id=1, source_target_pairs={{0,16},{16,32},{32,48},{48,64},{64,80},{80,96},{96,112},{112,128},... | collective-permute-start | bytes 786440 | tf_op jit(solution)/shard_map/while/body/eval_jaxpr/ppermute | solution.py:20
  315.9 13.4 %collective-permute-start = (f32[8,8192]{1,0:T(8,128)}, f32[8,8192]{1,0:T(8,128)S(1)}, u32[]{:S(2)}, u32[]{:S(2)}) collective-permute-start(f32[8,8192]{1,0:T(8,128)} %get-tuple-element.370), channel_id=1, source_target_pairs={{0,16},{16,32},{32,48},{48,64},{64,80},{80,96},{96,112},{112,128},... | collective-permute-start | bytes 786440 | tf_op jit(solution)/shard_map/while/body/eval_jaxpr/ppermute | solution.py:20
  331.0 12.6 %collective-permute-start = (f32[8,8192]{1,0:T(8,128)}, f32[8,8192]{1,0:T(8,128)S(1)}, u32[]{:S(2)}, u32[]{:S(2)}) collective-permute-start(f32[8,8192]{1,0:T(8,128)} %get-tuple-element.370), channel_id=1, source_target_pairs={{0,16},{16,32},{32,48},{48,64},{64,80},{80,96},{96,112},{112,128},... | collective-permute-start | bytes 786440 | tf_op jit(solution)/shard_map/while/body/eval_jaxpr/ppermute | solution.py:20
  414.1 12.1 %collective-permute-start = (f32[8,8192]{1,0:T(8,128)}, f32[8,8192]{1,0:T(8,128)S(1)}, u32[]{:S(2)}, u32[]{:S(2)}) collective-permute-start(f32[8,8192]{1,0:T(8,128)} %get-tuple-element.370), channel_id=1, source_target_pairs={{0,16},{16,32},{32,48},{48,64},{64,80},{80,96},{96,112},{112,128},... | collective-permute-start | bytes 786440 | tf_op jit(solution)/shard_map/while/body/eval_jaxpr/ppermute | solution.py:20
  427.8 12.4 %collective-permute-start = (f32[8,8192]{1,0:T(8,128)}, f32[8,8192]{1,0:T(8,128)S(1)}, u32[]{:S(2)}, u32[]{:S(2)}) collective-permute-start(f32[8,8192]{1,0:T(8,128)} %get-tuple-element.370), channel_id=1, source_target_pairs={{0,16},{16,32},{32,48},{48,64},{64,80},{80,96},{96,112},{112,128},... | collective-permute-start | bytes 786440 | tf_op jit(solution)/shard_map/while/body/eval_jaxpr/ppermute | solution.py:20
  441.9 13.5 %collective-permute-start = (f32[8,8192]{1,0:T(8,128)}, f32[8,8192]{1,0:T(8,128)S(1)}, u32[]{:S(2)}, u32[]{:S(2)}) collective-permute-start(f32[8,8192]{1,0:T(8,128)} %get-tuple-element.370), channel_id=1, source_target_pairs={{0,16},{16,32},{32,48},{48,64},{64,80},{80,96},{96,112},{112,128},... | collective-permute-start | bytes 786440 | tf_op jit(solution)/shard_map/while/body/eval_jaxpr/ppermute | solution.py:20
  457.0 14.7 %collective-permute-start = (f32[8,8192]{1,0:T(8,128)}, f32[8,8192]{1,0:T(8,128)S(1)}, u32[]{:S(2)}, u32[]{:S(2)}) collective-permute-start(f32[8,8192]{1,0:T(8,128)} %get-tuple-element.370), channel_id=1, source_target_pairs={{0,16},{16,32},{32,48},{48,64},{64,80},{80,96},{96,112},{112,128},... | collective-permute-start | bytes 786440 | tf_op jit(solution)/shard_map/while/body/eval_jaxpr/ppermute | solution.py:20
  473.4 14.0 %collective-permute-start = (f32[8,8192]{1,0:T(8,128)}, f32[8,8192]{1,0:T(8,128)S(1)}, u32[]{:S(2)}, u32[]{:S(2)}) collective-permute-start(f32[8,8192]{1,0:T(8,128)} %get-tuple-element.370), channel_id=1, source_target_pairs={{0,16},{16,32},{32,48},{48,64},{64,80},{80,96},{96,112},{112,128},... | collective-permute-start | bytes 786440 | tf_op jit(solution)/shard_map/while/body/eval_jaxpr/ppermute | solution.py:20
  489.1 13.2 %collective-permute-start = (f32[8,8192]{1,0:T(8,128)}, f32[8,8192]{1,0:T(8,128)S(1)}, u32[]{:S(2)}, u32[]{:S(2)}) collective-permute-start(f32[8,8192]{1,0:T(8,128)} %get-tuple-element.370), channel_id=1, source_target_pairs={{0,16},{16,32},{32,48},{48,64},{64,80},{80,96},{96,112},{112,128},... | collective-permute-start | bytes 786440 | tf_op jit(solution)/shard_map/while/body/eval_jaxpr/ppermute | solution.py:20
  503.9 12.3 %collective-permute-start = (f32[8,8192]{1,0:T(8,128)}, f32[8,8192]{1,0:T(8,128)S(1)}, u32[]{:S(2)}, u32[]{:S(2)}) collective-permute-start(f32[8,8192]{1,0:T(8,128)} %get-tuple-element.370), channel_id=1, source_target_pairs={{0,16},{16,32},{32,48},{48,64},{64,80},{80,96},{96,112},{112,128},... | collective-permute-start | bytes 786440 | tf_op jit(solution)/shard_map/while/body/eval_jaxpr/ppermute | solution.py:20
  518.0 12.1 %collective-permute-start = (f32[8,8192]{1,0:T(8,128)}, f32[8,8192]{1,0:T(8,128)S(1)}, u32[]{:S(2)}, u32[]{:S(2)}) collective-permute-start(f32[8,8192]{1,0:T(8,128)} %get-tuple-element.370), channel_id=1, source_target_pairs={{0,16},{16,32},{32,48},{48,64},{64,80},{80,96},{96,112},{112,128},... | collective-permute-start | bytes 786440 | tf_op jit(solution)/shard_map/while/body/eval_jaxpr/ppermute | solution.py:20
  531.7 12.1 %collective-permute-start = (f32[8,8192]{1,0:T(8,128)}, f32[8,8192]{1,0:T(8,128)S(1)}, u32[]{:S(2)}, u32[]{:S(2)}) collective-permute-start(f32[8,8192]{1,0:T(8,128)} %get-tuple-element.370), channel_id=1, source_target_pairs={{0,16},{16,32},{32,48},{48,64},{64,80},{80,96},{96,112},{112,128},... | collective-permute-start | bytes 786440 | tf_op jit(solution)/shard_map/while/body/eval_jaxpr/ppermute | solution.py:20
  545.5 12.1 %collective-permute-start = (f32[8,8192]{1,0:T(8,128)}, f32[8,8192]{1,0:T(8,128)S(1)}, u32[]{:S(2)}, u32[]{:S(2)}) collective-permute-start(f32[8,8192]{1,0:T(8,128)} %get-tuple-element.370), channel_id=1, source_target_pairs={{0,16},{16,32},{32,48},{48,64},{64,80},{80,96},{96,112},{112,128},... | collective-permute-start | bytes 786440 | tf_op jit(solution)/shard_map/while/body/eval_jaxpr/ppermute | solution.py:20
  559.2 12.1 %collective-permute-start = (f32[8,8192]{1,0:T(8,128)}, f32[8,8192]{1,0:T(8,128)S(1)}, u32[]{:S(2)}, u32[]{:S(2)}) collective-permute-start(f32[8,8192]{1,0:T(8,128)} %get-tuple-element.370), channel_id=1, source_target_pairs={{0,16},{16,32},{32,48},{48,64},{64,80},{80,96},{96,112},{112,128},... | collective-permute-start | bytes 786440 | tf_op jit(solution)/shard_map/while/body/eval_jaxpr/ppermute | solution.py:20
  600.5 12.6 %collective-permute-start = (f32[8,8192]{1,0:T(8,128)}, f32[8,8192]{1,0:T(8,128)S(1)}, u32[]{:S(2)}, u32[]{:S(2)}) collective-permute-start(f32[8,8192]{1,0:T(8,128)} %get-tuple-element.370), channel_id=1, source_target_pairs={{0,16},{16,32},{32,48},{48,64},{64,80},{80,96},{96,112},{112,128},... | collective-permute-start | bytes 786440 | tf_op jit(solution)/shard_map/while/body/eval_jaxpr/ppermute | solution.py:20
  614.8 13.7 %collective-permute-start = (f32[8,8192]{1,0:T(8,128)}, f32[8,8192]{1,0:T(8,128)S(1)}, u32[]{:S(2)}, u32[]{:S(2)}) collective-permute-start(f32[8,8192]{1,0:T(8,128)} %get-tuple-element.370), channel_id=1, source_target_pairs={{0,16},{16,32},{32,48},{48,64},{64,80},{80,96},{96,112},{112,128},... | collective-permute-start | bytes 786440 | tf_op jit(solution)/shard_map/while/body/eval_jaxpr/ppermute | solution.py:20
  630.2 14.9 %collective-permute-start = (f32[8,8192]{1,0:T(8,128)}, f32[8,8192]{1,0:T(8,128)S(1)}, u32[]{:S(2)}, u32[]{:S(2)}) collective-permute-start(f32[8,8192]{1,0:T(8,128)} %get-tuple-element.370), channel_id=1, source_target_pairs={{0,16},{16,32},{32,48},{48,64},{64,80},{80,96},{96,112},{112,128},... | collective-permute-start | bytes 786440 | tf_op jit(solution)/shard_map/while/body/eval_jaxpr/ppermute | solution.py:20
  646.8 14.0 %collective-permute-start = (f32[8,8192]{1,0:T(8,128)}, f32[8,8192]{1,0:T(8,128)S(1)}, u32[]{:S(2)}, u32[]{:S(2)}) collective-permute-start(f32[8,8192]{1,0:T(8,128)} %get-tuple-element.370), channel_id=1, source_target_pairs={{0,16},{16,32},{32,48},{48,64},{64,80},{80,96},{96,112},{112,128},... | collective-permute-start | bytes 786440 | tf_op jit(solution)/shard_map/while/body/eval_jaxpr/ppermute | solution.py:20
  662.5 13.2 %collective-permute-start = (f32[8,8192]{1,0:T(8,128)}, f32[8,8192]{1,0:T(8,128)S(1)}, u32[]{:S(2)}, u32[]{:S(2)}) collective-permute-start(f32[8,8192]{1,0:T(8,128)} %get-tuple-element.370), channel_id=1, source_target_pairs={{0,16},{16,32},{32,48},{48,64},{64,80},{80,96},{96,112},{112,128},... | collective-permute-start | bytes 786440 | tf_op jit(solution)/shard_map/while/body/eval_jaxpr/ppermute | solution.py:20
  677.3 12.3 %collective-permute-start = (f32[8,8192]{1,0:T(8,128)}, f32[8,8192]{1,0:T(8,128)S(1)}, u32[]{:S(2)}, u32[]{:S(2)}) collective-permute-start(f32[8,8192]{1,0:T(8,128)} %get-tuple-element.370), channel_id=1, source_target_pairs={{0,16},{16,32},{32,48},{48,64},{64,80},{80,96},{96,112},{112,128},... | collective-permute-start | bytes 786440 | tf_op jit(solution)/shard_map/while/body/eval_jaxpr/ppermute | solution.py:20
  691.3 12.1 %collective-permute-start = (f32[8,8192]{1,0:T(8,128)}, f32[8,8192]{1,0:T(8,128)S(1)}, u32[]{:S(2)}, u32[]{:S(2)}) collective-permute-start(f32[8,8192]{1,0:T(8,128)} %get-tuple-element.370), channel_id=1, source_target_pairs={{0,16},{16,32},{32,48},{48,64},{64,80},{80,96},{96,112},{112,128},... | collective-permute-start | bytes 786440 | tf_op jit(solution)/shard_map/while/body/eval_jaxpr/ppermute | solution.py:20
  (12 other events, 321.7 us)
Sparse Core Ops, SparseCore 0:
  10.4 195.7 all-gather.3
  220.7 37.8 all-reduce.4
where the time goes:
time: 741 us; the launch traced here: 739 us
  waiting for transfers between devices  570 us (77%)
  starting transfers between devices  62.2 us (8%)
  other arithmetic  58.5 us (8%)
  matrix products  16.5 us (2%)
  between operations  14.2 us (2%)
  blocking collectives  10.4 us (1%)
    ppermute x31, waiting for transfers between devices, passed_along(): return lax.ppermute(value, axis, pairs)  334 us
    all_gather x1, waiting for transfers between devices, shards(): piece = lax.all_gather(references, 'img', axis=0, tiled=True)  199 us
    ppermute x31, starting transfers between devices, passed_along(): return lax.ppermute(value, axis, pairs)  62.2 us
    add x31, other arithmetic, forward_turn(): return moved + slice_for(-1 - turn_index)  52.1 us
    psum x1, waiting for transfers between devices, shards(): scores = lax.psum(piece_scores, 'comp')  36 us
  transfers between devices with their start and end apart: 33, of which 33 were waited for; matrix products, arithmetic and copies ran while one was open for 0% of the time, Pallas kernels for 0%

commit v1 on v0

v1 whole, which is shorter than its diff:
```python
import jax
import jax.numpy as jnp
from jax import lax
from jax.sharding import Mesh, PartitionSpec as P

HIGHEST = lax.Precision.HIGHEST
PLANE = ("core", "yl", "x")
OWNERS = ("yh", "x", "core")
CHUNKS = (64, 32)


def shards(images, references):
    count_z = lax.axis_size("z")
    slices = lax.axis_size("x") * lax.axis_size("core")
    width = images.shape[1] // slices
    mine = lax.axis_index(("x", "core"))
    own = lax.dynamic_slice_in_dim(images, mine * width, width, 1)

    pieces = references.reshape(references.shape[0], slices, width).transpose(1, 0, 2)
    half = lax.all_to_all(pieces, ("x", "core"), 0, 0, tiled=True)
    plane_refs = lax.all_gather(half, "yh").reshape(-1, width)
    halfnorm = 0.5 * jnp.sum(plane_refs * plane_refs, axis=1)

    def scores_of(gathered):
        partial = lax.dot_general(
            gathered.reshape(-1, width), plane_refs, (((1,), (1,)), ((), ())),
            precision=HIGHEST, preferred_element_type=jnp.float32)
        partial = (partial - halfnorm[None, :]).reshape(count_z, -1, plane_refs.shape[0])
        return jnp.sum(lax.all_to_all(partial, PLANE, 0, 0, tiled=False), axis=0)

    def posterior_of(scores):
        largest = jnp.max(scores, axis=1)
        expon = jnp.exp(scores - largest[:, None])
        totals = jnp.sum(expon, axis=1)
        stats = jnp.stack([largest, totals])
        everyone = lax.all_to_all(
            jnp.broadcast_to(stats[None], (count_z,) + stats.shape), "z", 0, 0, tiled=False)
        top = jnp.max(everyone[:, 0], axis=0)
        total = jnp.sum(everyone[:, 1] * jnp.exp(everyone[:, 0] - top), axis=0)
        post = expon * (jnp.exp(largest - top) / total)[:, None]
        chips = lax.axis_size("yl") * lax.axis_size("x")
        spread = lax.all_to_all(
            jnp.broadcast_to(post[None], (chips,) + post.shape), ("yl", "x"), 0, 0, tiled=False)
        return lax.all_gather(spread, "core").reshape(-1, post.shape[1])

    out = None
    start = 0
    for rows in CHUNKS:
        part = lax.slice_in_dim(own, start, start + rows, axis=0)
        start += rows
        gathered = lax.all_gather(part, "z")
        post = posterior_of(scores_of(gathered))
        term = lax.dot_general(
            post, gathered.reshape(-1, width), (((0,), (0,)), ((), ())),
            precision=HIGHEST, preferred_element_type=jnp.float32)
        out = term if out is None else out + term

    owners = lax.axis_size("yh") * slices
    back = lax.all_to_all(out.reshape(owners, -1, width), OWNERS, 0, 0, tiled=False)
    rows = jnp.sum(back.reshape(lax.axis_size("yh"), slices, -1, width), axis=0)
    return rows.transpose(1, 0, 2).reshape(references.shape)


def solution(mesh):
    fine = Mesh(mesh.devices.reshape(16, 2, 2, 4, 2), ("z", "yh", "yl", "x", "core"))
    return jax.shard_map(
        shards,
        mesh=fine,
        in_specs=(P(("z", "yh"), "yl"), P(("z", "yh", "x", "core"), "yl")),
        out_specs=P(("z", "yh", "x", "core"), "yl"),
        check_vma=False,
    )
```

time: 741 us -> 262 us (0.35)
  waiting for transfers between devices: 570 us -> 121 us
  blocking collectives: 10.4 us -> 75.9 us
  other arithmetic: 58.5 us -> 2.47 us
  starting transfers between devices: 62.2 us -> 24.1 us
    ppermute x31 -> x0, waiting for transfers between devices: 334 us -> none  [passed_along(): return lax.ppermute(value, axis, pairs)]
    all_gather x1 -> x2, waiting for transfers between devices: 199 us -> 94.3 us  [shards(): gathered = lax.all_gather(part, 'z')]
    ppermute x31 -> x0, starting transfers between devices: 62.2 us -> none  [passed_along(): return lax.ppermute(value, axis, pairs)]
    all_to_all x0 -> x4, blocking collectives: none -> 61.9 us  [the longest x1 19.9 us: posterior_of(): lax.all_to_all(jnp.broadcast_to(stats[None], (count_z,) + stats.shape), '...]
    add x38 -> x0, other arithmetic: 52.3 us -> none  [the longest x31 52.1 us: forward_turn(): return moved + slice_for(-1 - turn_index)]
    psum x1 -> x0, waiting for transfers between devices: 36 us -> none  [shards(): scores = lax.psum(piece_scores, 'comp')]
    all_to_all x0 -> x4, waiting for transfers between devices: none -> 26.2 us  [the longest x1 10.4 us: posterior_of(): lax.all_to_all(jnp.broadcast_to(stats[None], (count_z,) + stats.shape), '...]
    all_to_all x0 -> x4, starting transfers between devices: none -> 24.1 us  [the longest x2 11 us: posterior_of(): lax.all_to_all(jnp.broadcast_to(post[None], (chips,) + post.shape), ('yl'...]
  transfers between devices with their start and end apart: 33 -> 6, of which waited for: 33 -> 6; matrix products, arithmetic and copies ran while one was open for 0% -> 3% of each run, Pallas kernels for 0% -> 0%
where the time goes in v1:
time: 262 us; the launch traced here: 258 us
  waiting for transfers between devices  121 us (46%)
  blocking collectives  75.9 us (29%)
  starting transfers between devices  24.1 us (9%)
  matrix products  15.8 us (6%)
  between operations  13.5 us (5%)
  local copies, waits for them, and re-layouts  6.02 us (2%)
    all_gather x2, waiting for transfers between devices, shards(): gathered = lax.all_gather(part, 'z')  94.3 us
    all_to_all x1, blocking collectives, posterior_of(): lax.all_to_all(jnp.broadcast_to(stats[None], (count_z,) + stats.shape), '...  19.9 us
    all_to_all x1, blocking collectives, shards(): lax.all_to_all(out.reshape(owners, -1, width), OWNERS, 0, 0, tiled=False)  16 us
    all_to_all x1, blocking collectives, shards(): half = lax.all_to_all(pieces, ('x', 'core'), 0, 0, tiled=True)  14.6 us
    all_to_all x1, blocking collectives, scores_of(): return jnp.sum(lax.all_to_all(partial, PLANE, 0, 0, tiled=False), axis=0)  11.4 us
    all_to_all x2, starting transfers between devices, posterior_of(): lax.all_to_all(jnp.broadcast_to(post[None], (chips,) + post.shape), ('yl'...  11 us
    all_to_all x1, waiting for transfers between devices, posterior_of(): lax.all_to_all(jnp.broadcast_to(stats[None], (count_z,) + stats.shape), '...  10.4 us
    all_gather x1, blocking collectives, shards(): plane_refs = lax.all_gather(half, 'yh').reshape(-1, width)  9.84 us
  transfers between devices with their start and end apart: 6, of which 6 were waited for; matrix products, arithmetic and copies ran while one was open for 3% of the time, Pallas kernels for 0%

profile of v1, /device:TPU:6, one launch (start us, length us, event | category | flops | bytes accessed | tf_op | source)
XLA Modules:
  0.0 258.3 jit_solution(16840067676894217724)
XLA Ops:
  6.5 1.6 dynamic-slice.1
  8.2 1.7 constant_dynamic-slice_fusion
  9.9 14.6 %all_to_all.40 = f32[8,8,1024]{2,1,0:T(8,128)S(1)} all-to-all(f32[8,8,1024]{2,1,0:T(8,128)} %bitcast.40), channel_id=1, replica_groups=mesh['z'=16,'yh'=2,'yl'=2,'x'=4,'core'=2] {'x','core'}, dimensions={0} | all-to-all | bytes 524288 | tf_op jit(solution)/shard_map/all_to_all | solution.py:20
  24.5 9.8 %all-gather.1 = f32[16,8,1024]{2,1,0:T(8,128)S(1)} all-gather(f32[8,8,1024]{2,1,0:T(8,128)S(1)} %all_to_all.40), channel_id=3, replica_groups=mesh['z'=16,'yh'=2,'yl'=2,'x'=4,'core'=2] {'yh'}, dimensions={0}, use_global_device_ids=true | all-gather | bytes 786432 | tf_op jit(solution)/shard_map/all_gather | solution.py:21
  34.5 52.0 %all-gather.10.cloned.1.call-done = f32[512,1024]{1,0:T(8,128)} async-done(((f32[32,1024]{1,0:T(8,128)}), f32[512,1024]{1,0:T(8,128)}) %all-gather.10.cloned.1.call-update) | async-done | bytes 2097168 | tf_op jit(solution)/shard_map/all_gather | solution.py:51
  86.5 3.4 %convolution_subtract_fusion.1 = f32[512,128]{1,0:T(8,128)S(1)} fusion(f32[512,1024]{1,0:T(8,128)} %all-gather.10.cloned.1.call-done, f32[16,8,1024]{2,1,0:T(8,128)S(1)} %all-gather.1, f32[128]{0:T(128)S(1)} %mul.58), kind=kOutput, calls=%fused_computation.3 | convolution fusion | flops 805371904 | bytes 2884096 | tf_op jit(solution)/shard_map/dot_general | solution.py:25
  89.9 11.4 %all_to_all.41 = f32[16,32,128]{2,1,0:T(8,128)S(1)} all-to-all(f32[16,32,128]{2,1,0:T(8,128)S(1)} %bitcast.38), channel_id=1, replica_groups=mesh['z'=16,'yh'=2,'yl'=2,'x'=4,'core'=2] {'core','yl','x'}, dimensions={0} | all-to-all | bytes 524288 | tf_op jit(solution)/shard_map/all_to_all | solution.py:29
  101.7 19.9 %all_to_all.42 = f32[16,2,32]{2,1,0:T(2,128)S(1)} all-to-all(f32[16,2,32]{2,1,0:T(2,128)S(1)} %broadcast_in_dim.10), channel_id=1, replica_groups=mesh['z'=16,'yh'=2,'yl'=2,'x'=4,'core'=2] {'z'}, dimensions={0} | all-to-all | bytes 8192 | tf_op jit(solution)/shard_map/all_to_all | solution.py:36
  121.6 42.3 %all-gather.8.cloned.1.call-done = f32[1024,1024]{1,0:T(8,128)} async-done(((f32[64,1024]{1,0:T(8,128)}), f32[1024,1024]{1,0:T(8,128)}) %all-gather.8.cloned.1.call-update) | async-done | bytes 4194320 | tf_op jit(solution)/shard_map/all_gather | solution.py:51
  163.9 6.4 %convolution_subtract_fusion = f32[1024,128]{1,0:T(8,128)} fusion(f32[1024,1024]{1,0:T(8,128)} %all-gather.8.cloned.1.call-done, f32[16,8,1024]{2,1,0:T(8,128)S(1)} %all-gather.1, f32[128]{0:T(128)S(1)} %mul.58), kind=kOutput, calls=%fused_computation.1 | convolution fusion | flops 1610743808 | bytes 5243392 | tf_op jit(solution)/shard_map/dot_general | solution.py:25
  170.3 6.0 %all-to-all-start.1 = ((f32[16,64,128]{2,1,0:T(8,128)}), f32[16,64,128]{2,1,0:T(8,128)S(1)}, u32[]{:S(2)}, u32[]{:S(2)}) async-start(f32[16,64,128]{2,1,0:T(8,128)} %bitcast.3), calls=%async_computation.1 | async-start | bytes 1048576 | tf_op jit(solution)/shard_map/all_to_all | solution.py:29
  176.5 8.2 %all-to-all-done.1 = f32[16,64,128]{2,1,0:T(8,128)S(1)} async-done(((f32[16,64,128]{2,1,0:T(8,128)}), f32[16,64,128]{2,1,0:T(8,128)S(1)}, u32[]{:S(2)}, u32[]{:S(2)}) %all-to-all-start.1) | async-done | bytes 524320 | tf_op jit(solution)/shard_map/all_to_all | solution.py:29
  185.3 5.7 %all-to-all-start.6 = ((f32[8,32,128]{2,1,0:T(8,128)}), f32[8,32,128]{2,1,0:T(8,128)S(1)}, u32[]{:S(2)}, u32[]{:S(2)}) async-start(f32[8,32,128]{2,1,0:T(8,128)} %broadcast_in_dim.11), calls=%async_computation.6 | async-start | bytes 262144 | tf_op jit(solution)/shard_map/all_to_all | solution.py:42
  192.0 3.7 %all-to-all-done.6 = f32[8,32,128]{2,1,0:T(8,128)S(1)} async-done(((f32[8,32,128]{2,1,0:T(8,128)}), f32[8,32,128]{2,1,0:T(8,128)S(1)}, u32[]{:S(2)}, u32[]{:S(2)}) %all-to-all-start.6) | async-done | bytes 131104 | tf_op jit(solution)/shard_map/all_to_all | solution.py:42
  195.7 7.1 %all-to-all-start.2 = ((f32[16,1,128]{2,1,0:T(1,128)}), f32[16,1,128]{2,1,0:T(1,128)S(1)}, u32[]{:S(2)}, u32[]{:S(2)}) async-start(f32[16,1,128]{2,1,0:T(1,128)} %reshape.148), calls=%async_computation.2 | async-start | bytes 16384 | tf_op jit(solution)/shard_map/all_to_all | solution.py:36
  202.8 2.0 all-gather.4
  204.8 10.4 %all-to-all-done.2 = f32[16,1,128]{2,1,0:T(1,128)S(1)} async-done(((f32[16,1,128]{2,1,0:T(1,128)}), f32[16,1,128]{2,1,0:T(1,128)S(1)}, u32[]{:S(2)}, u32[]{:S(2)}) %all-to-all-start.2) | async-done | bytes 8224 | tf_op jit(solution)/shard_map/all_to_all | solution.py:36
  217.4 5.3 %all-to-all-start.3 = ((f32[8,64,128]{2,1,0:T(8,128)}), f32[8,64,128]{2,1,0:T(8,128)S(1)}, u32[]{:S(2)}, u32[]{:S(2)}) async-start(f32[8,64,128]{2,1,0:T(8,128)} %broadcast_in_dim.9), calls=%async_computation.3 | async-start | bytes 524288 | tf_op jit(solution)/shard_map/all_to_all | solution.py:42
  222.7 1.3 fusion.9
  224.0 3.9 %all-to-all-done.3 = f32[8,64,128]{2,1,0:T(8,128)S(1)} async-done(((f32[8,64,128]{2,1,0:T(8,128)}), f32[8,64,128]{2,1,0:T(8,128)S(1)}, u32[]{:S(2)}, u32[]{:S(2)}) %all-to-all-start.3) | async-done | bytes 262176 | tf_op jit(solution)/shard_map/all_to_all | solution.py:42
  227.9 2.2 all-gather.2
  230.0 4.7 %fusion = f32[16,8,1024]{2,1,0:T(8,128)S(1)} fusion(f32[128,1024]{1,0:T(8,128)S(1)} %fusion.9, f32[1024,128]{1,0:T(8,128)S(1)} %bitcast.37, f32[1024,1024]{1,0:T(8,128)} %all-gather.8.cloned.1.call-done), kind=kOutput, calls=%fused_computation.2 | convolution fusion | flops 1610743808 | bytes 5767168 | tf_op jit(solution)/shard_map/dot_general | solution.py:53
  234.7 16.0 %all_to_all.43 = f32[16,8,1024]{2,1,0:T(8,128)S(1)} all-to-all(f32[16,8,1024]{2,1,0:T(8,128)S(1)} %fusion), channel_id=1, replica_groups=mesh['z'=16,'yh'=2,'yl'=2,'x'=4,'core'=2] {'yh','x','core'}, dimensions={0} | all-to-all | bytes 1048576 | tf_op jit(solution)/shard_map/all_to_all | solution.py:59
  250.7 0.7 reduce_sum.79
  (35 shorter events, 4.6 us)
Async XLA Ops:
  6.5 79.9 %all-gather.10.cloned.1.call-start = ((), (), s32[]{:S(2)}) async-start(), calls=%async_computation.9 | async-start | bytes 2228224 | tf_op jit(solution)/shard_map/all_gather | solution.py:51
  8.1 155.8 %all-gather.8.cloned.1.call-start = ((), (), s32[]{:S(2)}) async-start(), calls=%async_computation.8 | async-start | bytes 4456448 | tf_op jit(solution)/shard_map/all_gather | solution.py:51
  121.6 101.1 %copy-start = (f32[512,1024]{1,0:T(8,128)S(1)}, f32[512,1024]{1,0:T(8,128)}, u32[]{:S(2)}) copy-start(f32[512,1024]{1,0:T(8,128)} %all-gather.10.cloned.1.call-done) | copy-start | bytes 6291460
  170.3 14.3 %all-to-all-start.1 = ((f32[16,64,128]{2,1,0:T(8,128)}), f32[16,64,128]{2,1,0:T(8,128)S(1)}, u32[]{:S(2)}, u32[]{:S(2)}) async-start(f32[16,64,128]{2,1,0:T(8,128)} %bitcast.3), calls=%async_computation.1 | async-start | bytes 1048576 | tf_op jit(solution)/shard_map/all_to_all | solution.py:29
  185.3 10.5 %all-to-all-start.6 = ((f32[8,32,128]{2,1,0:T(8,128)}), f32[8,32,128]{2,1,0:T(8,128)S(1)}, u32[]{:S(2)}, u32[]{:S(2)}) async-start(f32[8,32,128]{2,1,0:T(8,128)} %broadcast_in_dim.11), calls=%async_computation.6 | async-start | bytes 262144 | tf_op jit(solution)/shard_map/all_to_all | solution.py:42
  195.7 19.5 %all-to-all-start.2 = ((f32[16,1,128]{2,1,0:T(1,128)}), f32[16,1,128]{2,1,0:T(1,128)S(1)}, u32[]{:S(2)}, u32[]{:S(2)}) async-start(f32[16,1,128]{2,1,0:T(1,128)} %reshape.148), calls=%async_computation.2 | async-start | bytes 16384 | tf_op jit(solution)/shard_map/all_to_all | solution.py:36
  217.4 10.5 %all-to-all-start.3 = ((f32[8,64,128]{2,1,0:T(8,128)}), f32[8,64,128]{2,1,0:T(8,128)S(1)}, u32[]{:S(2)}, u32[]{:S(2)}) async-start(f32[8,64,128]{2,1,0:T(8,128)} %broadcast_in_dim.9), calls=%async_computation.3 | async-start | bytes 524288 | tf_op jit(solution)/shard_map/all_to_all | solution.py:42
Sparse Core Ops, SparseCore 0:
  9.4 77.0 all-gather.9
  88.5 75.3 all-gather.7
